TPU v7x, 32 devices: a whole 2x2x4 slice. The times are simulated.
32 devices in a mesh: island: 8 (over z, x), mp: 4 (over y, core).
Axes of the slice: x: 2, y: 2, z: 4, core: 2. Of those that a mesh axis runs over, the one named last changes fastest.
Arguments:
- acts: bfloat16 [8, 1024, 8192], P('island', None, 'mp'), may hold values from -6 to 6
- queries: bfloat16 [8, 1024, 4096], P('island', None, 'mp'), may hold values from -41 to 41
- keys_values: bfloat16 [8, 1024, 1024], P('island', 'mp'), may hold values from -4 to 4
- out_grad: bfloat16 [8, 1024, 4096], P('island', None, 'mp'), may hold values from -6 to 6
- segments: int32 [8, 1024], P('island'), may hold values from 0 to 15, never falling along the last dimension, each value on 1 to 512 neighbouring positions
- drift: bfloat16 [8, 8192, 1024], P('island', 'mp'), may hold values from -1.1953125 to 1.1953125
- outer_weights: float32 [4, 2048, 1024], P('mp', 'island'), may hold values from -6 to 6
- momentum: float32 [4, 2048, 1024], P('mp', 'island'), may hold values from -1.2 to 1.2
Outputs:
- query_grads: bfloat16 [8, 1024, 4096], P('island', None, 'mp')
- new_outer: float32 [4, 2048, 1024], P('mp', 'island')
- new_momentum: float32 [4, 2048, 1024], P('mp', 'island')
- next_weights: bfloat16 [4, 2048, 1024], P('mp')
Inputs may be any that keep to these rules, and one draw needn't show every extreme that they name: `segments`: document ids never fall along a sequence.
All inputs are finite; a program needn't handle non-finite values.
Results may differ from a plain program's by a relative error of at most 0.0085.
Values may be sent and summed in bfloat16 or wider, within the bound.
No kernel may reach another device: no remote copies, remote signals or barrier semaphores. Data moves between devices by JAX's collectives and lax.ppermute only.
A program may use at most 192 MiB of HBM per device.

v0:
```python
import math
import jax
import jax.numpy as jnp
from jax import lax
from jax.sharding import PartitionSpec as P

D = 8192
HD = 128
QH = 32
KVH = 4
INNER_LR = 0.8
OUTER_LR = 0.7
MOMENTUM = 0.9
ROPE_BASE = 500000.0


def rope_tables(positions, head_width):
    half_width = head_width // 2
    exponent = jnp.arange(half_width, dtype=jnp.float32) * (2.0 / head_width)
    frequency = jnp.power(jnp.float32(ROPE_BASE), -exponent)
    angles = jnp.arange(positions, dtype=jnp.float32)[:, None] * frequency[None, :]
    return (jnp.cos(angles), jnp.sin(angles))


def unrotate(grads, cosine, sine_table):
    half_width = grads.shape[-1] // 2
    first_half = grads[..., :half_width]
    second_half = grads[..., half_width:]
    cos_wide = cosine[:, None, :]
    sin_wide = sine_table[:, None, :]
    return jnp.concatenate(
        [
            first_half * cos_wide + second_half * sin_wide,
            second_half * cos_wide - first_half * sin_wide,
        ],
        axis=-1,
    )


def attention_probs(query_rows, key_cols, segment_ids, score_scale):
    positions = jnp.arange(segment_ids.shape[0])
    allowed = (positions[:, None] >= positions[None, :]) & (
        segment_ids[:, None] == segment_ids[None, :]
    )
    scores = (
        jnp.einsum("qhd,kd->hqk", query_rows, key_cols, preferred_element_type=jnp.float32)
        * score_scale
    )
    scores = jnp.where(allowed[None], scores, -jnp.inf)
    shifted = scores - jnp.max(scores, axis=-1, keepdims=True)
    weights = jnp.exp(shifted)
    attn_probs = weights / jnp.sum(weights, axis=-1, keepdims=True)
    return (attn_probs, attn_probs.astype(jnp.bfloat16))


def value_part(probs_low, grad_rows):
    return jnp.einsum("hqk,qhd->kd", probs_low, grad_rows, preferred_element_type=jnp.float32)


def score_part(attn_probs, query_rows, key_cols, value_cols, grad_rows, score_scale):
    dprobs = jnp.einsum("qhd,kd->hqk", grad_rows, value_cols, preferred_element_type=jnp.float32)
    row_dot = jnp.sum(attn_probs * dprobs, axis=-1, keepdims=True)
    dscores = (attn_probs * (dprobs - row_dot)).astype(jnp.bfloat16)
    query_grads = (
        jnp.einsum("hqk,kd->qhd", dscores, key_cols, preferred_element_type=jnp.float32)
        * score_scale
    ).astype(jnp.bfloat16)
    key_grads = (
        jnp.einsum("hqk,qhd->kd", dscores, query_rows, preferred_element_type=jnp.float32)
        * score_scale
    )
    return (query_grads, key_grads)


def fold_heads(received, mp_count):
    block_rows = received.shape[0] // mp_count
    return jnp.sum(received.reshape(KVH, mp_count // KVH, block_rows, received.shape[1]), axis=1)


def head_major(folded):
    return jnp.transpose(folded, (1, 0, 2))


def weight_grad(acts_rows, grads_low, inv_width):
    return (
        lax.dot_general(
            acts_rows, grads_low, (((0,), (0,)), ((), ())), preferred_element_type=jnp.float32
        )
        * inv_width
    )


def sum_values(value_piece, half_kv, mp_count):
    tok_count = value_piece.shape[0]
    block_rows = tok_count // mp_count
    value_received = lax.all_to_all(
        value_piece.astype(jnp.bfloat16), "mp", split_axis=0, concat_axis=0, tiled=True
    ).astype(value_piece.dtype)
    value_block = head_major(fold_heads(value_received, mp_count)).reshape(block_rows, half_kv)
    return lax.all_gather(value_block.astype(jnp.bfloat16), "mp", axis=0, tiled=True)


def sum_keys(key_piece, half_kv, mp_count, cos_block, sin_block):
    tok_count = key_piece.shape[0]
    block_rows = tok_count // mp_count
    key_received = lax.all_to_all(
        key_piece.astype(jnp.bfloat16), "mp", split_axis=0, concat_axis=0, tiled=True
    ).astype(key_piece.dtype)
    key_block = head_major(fold_heads(key_received, mp_count))
    key_plain = unrotate(key_block, cos_block, sin_block).reshape(block_rows, half_kv)
    return lax.all_gather(key_plain.astype(jnp.bfloat16), "mp", axis=0, tiled=True)


def body(acts, queries, keys_values, out_grad, segments, drift, outer_weights, momentum):
    acts_rows = acts[0]
    tok_count = acts_rows.shape[0]
    island_count = lax.axis_size("island")
    mp_count = lax.axis_size("mp")
    block_rows = tok_count // mp_count
    head_dim = HD
    local_heads = queries.shape[2] // head_dim
    kv_width = keys_values.shape[2]
    half_kv = kv_width // 2
    group_size = QH // KVH
    score_scale = 1.0 / math.sqrt(head_dim)
    inv_width = 1.0 / math.sqrt(D)
    kv_index = lax.axis_index("mp") * local_heads // group_size
    block_start = lax.axis_index("mp") * block_rows
    gathered = lax.all_gather(keys_values, "mp", axis=1, tiled=True)[0]
    key_cols = lax.dynamic_slice_in_dim(gathered, kv_index * head_dim, head_dim, 1)
    value_cols = lax.dynamic_slice_in_dim(gathered, half_kv + kv_index * head_dim, head_dim, 1)
    query_rows = queries[0].reshape(tok_count, local_heads, head_dim)
    grad_rows = out_grad[0].reshape(tok_count, local_heads, head_dim)
    segment_ids = segments[0]
    cosine, sine_table = rope_tables(tok_count, head_dim)
    cos_block = lax.dynamic_slice_in_dim(cosine, block_start, block_rows, 0)
    sin_block = lax.dynamic_slice_in_dim(sine_table, block_start, block_rows, 0)
    drift_rows = drift[0]
    attn_probs, probs_low = attention_probs(query_rows, key_cols, segment_ids, score_scale)
    value_piece = value_part(probs_low, grad_rows)
    value_low = sum_values(value_piece, half_kv, mp_count)
    query_grads, key_piece = score_part(
        attn_probs, query_rows, key_cols, value_cols, grad_rows, score_scale
    )
    key_low = sum_keys(key_piece, half_kv, mp_count, cos_block, sin_block)
    grads_low = jnp.concatenate([key_low, value_low], axis=1)
    island_terms = drift_rows.astype(jnp.float32) - INNER_LR * weight_grad(
        acts_rows, grads_low, inv_width
    )
    reduced = lax.psum_scatter(
        island_terms.astype(jnp.bfloat16), "island", scatter_dimension=0, tiled=True
    ).astype(jnp.float32)
    outer_grad = -(reduced / island_count)
    new_momentum = MOMENTUM * momentum[0] + outer_grad
    new_outer = outer_weights[0] - OUTER_LR * (outer_grad + MOMENTUM * new_momentum)
    next_weights = lax.all_gather(new_outer.astype(jnp.bfloat16), "island", axis=0, tiled=True)
    query_out = query_grads.reshape(tok_count, local_heads * head_dim)
    return (query_out[None], new_outer[None], new_momentum[None], next_weights[None])


def solution(mesh):
    in_specs = (
        P("island", None, "mp"),
        P("island", None, "mp"),
        P("island", "mp", None),
        P("island", None, "mp"),
        P("island", None),
        P("island", "mp", None),
        P("mp", "island", None),
        P("mp", "island", None),
    )
    out_specs = (
        P("island", None, "mp"),
        P("mp", "island", None),
        P("mp", "island", None),
        P("mp", None, None),
    )
    return jax.shard_map(body, mesh=mesh, in_specs=in_specs, out_specs=out_specs, check_vma=False)
```

profile of v0, /device:TPU:0, one launch (start us, length us, event | category | flops | bytes accessed | tf_op | source)
XLA Modules:
  0.0 354.0 jit_solution(6495769654644063635)
XLA Ops:
  7.2 0.0 copy-start
  7.2 0.0 all-gather.5.cloned.1.call-start
  7.2 0.7 all-gather.5.cloned.1.call-update
  7.9 0.0 copy-start.3
  7.9 3.5 %copy.43 = bf16[128,8,8,128]{3,2,1,0:T(8,128)(2,1)} copy(bf16[128,8,8,128]{3,1,2,0:T(8,128)(2,1)} %bitcast.103) | data formatting | bytes 4194304
  11.5 0.0 copy-done
  11.5 1.9 copy.44
  13.4 0.0 copy-done.3
  13.4 0.6 fusion.12
  14.1 20.8 %all-gather.5.cloned.1.call-done = bf16[1,1024,1024]{2,1,0:T(8,128)(2,1)} async-done(((bf16[1,256,1024]{2,1,0:T(8,128)(2,1)}), bf16[1,1024,1024]{2,1,0:T(8,128)(2,1)}) %all-gather.5.cloned.1.call-update) | async-done | bytes 2097168 | tf_op jit(solution)/shard_map/all_gather | solution.py:129
  34.9 0.0 copy-start.1
  34.9 19.1 %fusion.73 = (f32[8,1024]{1,0:T(8,128)S(1)}, f32[8,1024,1024]{1,2,0:T(8,128)}) fusion(pred[1024,1024]{0,1:T(8,128)(4,1)S(1)} %fusion.12, bf16[1024,8,128]{2,1,0:T(8,128)(2,1)} %bitcast.107, bf16[1,1024,1024]{2,1,0:T(8,128)(2,1)} %all-gather.5.cloned.1.call-done, s32[]{:T(128)S(6)} %select_n.20), kind=kOutput, calls=%fused_computation.67 | convolution fusion | flops 2181039104 | bytes 36995076 | tf_op jit(solution)/shard_map/sub | solution.py:50
  53.9 0.0 copy-done.1
  53.9 21.3 %fusion.1 = (f32[8,1024]{1,0:T(8,128)S(1)}, f32[1024,1024,8]{1,0,2:T(8,128)}) fusion(f32[8,1024,1024]{1,2,0:T(8,128)} %get-tuple-element.20, f32[8,1024]{1,0:T(8,128)S(1)} %get-tuple-element.19, bf16[1024,8,128]{2,1,0:T(8,128)(2,1)S(1)} %bitcast.105, bf16[1,1024,1024]{2,1,0:T(8,128)(2,1)} %all-gather.5.cloned.1.call-done, s32[]{:T(128)S(6)} %select_n.22), kind=kOutput, calls=%fused_computation.3 | convolution fusion | flops 2172641280 | bytes 69533696 | tf_op jit(solution)/shard_map/qhd,kd->hqk/dot_general | solution.py:61
  75.2 27.9 %fusion.3 = bf16[8,1024,1024]{1,2,0:T(8,128)(2,1)} fusion(f32[1024,1024,8]{1,0,2:T(8,128)} %get-tuple-element.22, f32[8,1024]{1,0:T(8,128)S(1)} %get-tuple-element.21, f32[8,1024,1024]{1,2,0:T(8,128)} %get-tuple-element.20, f32[8,1024]{1,0:T(8,128)S(1)} %get-tuple-element.19), kind=kLoop, calls=%fused_computation.5 | loop fusion | flops 33554432 | bytes 83951616 | tf_op jit(solution)/shard_map/convert_element_type | solution.py:63
  103.1 10.8 %fusion.41 = bf16[1024,128]{1,0:T(8,128)(2,1)S(1)} fusion(bf16[8,1024,1024]{1,2,0:T(8,128)(2,1)} %fusion.3, bf16[1024,8,128]{2,1,0:T(8,128)(2,1)} %bitcast.108), kind=kOutput, calls=%fused_computation.36 | convolution fusion | flops 2147745792 | bytes 19136512 | tf_op jit(solution)/shard_map/hqk,qhd->kd/dot_general | solution.py:69
  114.0 0.9 copy.32
  114.8 3.4 all-to-all-start
  118.3 0.2 all-gather.7.cloned.1.call-start
  118.5 0.1 iota_multiply_fusion
  118.6 0.2 dynamic-slice_cosine_fusion
  118.8 5.4 %all-to-all-done = bf16[4,256,128]{1,2,0:T(8,128)(2,1)S(1)} async-done(((bf16[4,256,128]{1,2,0:T(8,128)(2,1)}), bf16[4,256,128]{1,2,0:T(8,128)(2,1)S(1)}, u32[]{:S(2)}, u32[]{:S(2)}) %all-to-all-start) | async-done | bytes 262176 | tf_op jit(solution)/shard_map/all_to_all | solution.py:106
  124.3 0.1 add_convert_fusion
  124.3 0.7 pad_maximum_fusion
  125.1 0.0 all-gather.7.cloned.1.call-update
  125.1 0.0 all-gather.9.cloned.1.call-start
  125.1 13.3 %fusion.44 = bf16[1024,128]{1,0:T(8,128)(2,1)S(1)} fusion(bf16[1024,8,128]{2,1,0:T(8,128)(2,1)S(1)} %bitcast.106, f32[8,1024,1024]{1,2,0:T(8,128)} %get-tuple-element.20, f32[8,1024]{1,0:T(8,128)S(1)} %get-tuple-element.19), kind=kOutput, calls=%fused_computation.37 | convolution fusion | flops 2164391936 | bytes 35946496 | tf_op jit(solution)/shard_map/hqk,qhd->kd/dot_general | solution.py:57
  138.5 0.1 copy.34
  138.6 9.1 %all_to_all.18 = bf16[4,256,128]{1,2,0:T(8,128)(2,1)} all-to-all(bf16[4,256,128]{1,2,0:T(8,128)(2,1)S(1)} %copy.34), channel_id=1, replica_groups=mesh['island'=8,'mp'=4] {'mp'}, dimensions={0} | all-to-all | bytes 524288 | tf_op jit(solution)/shard_map/all_to_all | solution.py:96
  147.7 0.0 all-gather.9.cloned.1.call-update
  147.7 0.0 reduce-scatter.2.cloned.1.call-start
  147.8 6.4 %copy.30 = bf16[1,2048,1024]{1,2,0:T(8,128)(2,1)} copy(bf16[1,2048,1024]{2,1,0:T(8,128)(2,1)} %param.13) | data formatting | bytes 8388608 | tf_op args[5]
  154.2 0.0 all-gather.7.cloned.1.call-done
  154.2 10.5 %all-gather.9.cloned.1.call-done = bf16[1024,512]{0,1:T(8,128)(2,1)} async-done(((bf16[256,512]{0,1:T(8,128)(2,1)}), bf16[1024,512]{0,1:T(8,128)(2,1)}) %all-gather.9.cloned.1.call-update) | async-done | bytes 1048592 | tf_op jit(solution)/shard_map/all_gather | solution.py:100
  164.7 10.6 %fusion.10 = bf16[2048,1024]{0,1:T(8,128)(2,1)} fusion(bf16[1,2048,1024]{1,2,0:T(8,128)(2,1)} %copy.30, bf16[1,1024,2048]{2,1,0:T(8,128)(2,1)} %param.8, bf16[1024,512]{0,1:T(8,128)(2,1)} %all-gather.9.cloned.1.call-done, bf16[1024,512]{0,1:T(8,128)(2,1)} %all-gather.7.cloned.1.call-done), kind=kOutput, calls=%fused_computation.16 | convolution fusion | flops 4307550208 | bytes 14680064 | tf_op jit(solution)/shard_map/dot_general | solution.py:86
  175.3 0.0 copy-start.2
  175.3 0.0 reduce-scatter.2.cloned.1.call-update
  175.3 0.0 all-gather.11.cloned.1.call-start
  175.3 1.1 copy-done.2
  176.5 0.3 copy.29
  176.8 1.6 copy.35
  178.4 85.8 %reduce-scatter.2.cloned.1.call-done = bf16[256,1024]{0,1:T(8,128)(2,1)} async-done(((bf16[2048,1024]{0,1:T(8,128)(2,1)}), bf16[256,1024]{0,1:T(8,128)(2,1)}) %reduce-scatter.2.cloned.1.call-update) | async-done | bytes 524304 | tf_op jit(solution)/shard_map/reduce_scatter | solution.py:150
  264.2 2.5 fusion.71
  266.6 0.0 all-gather.11.cloned.1.call-update
  266.7 8.5 %multiply_convert_fusion = bf16[128,8,1024]{2,0,1:T(8,128)(2,1)S(1)} fusion(bf16[8,1024,1024]{1,2,0:T(8,128)(2,1)} %fusion.3, bf16[1,1024,1024]{2,1,0:T(8,128)(2,1)} %all-gather.5.cloned.1.call-done, s32[]{:T(128)S(6)} %select_n.20), kind=kOutput, calls=%fused_computation.18 | convolution fusion | flops 2149580800 | bytes 19136516 | tf_op jit(solution)/shard_map/hqk,kd->qhd/dot_general | solution.py:65
  275.2 2.6 copy.36
  277.8 2.5 copy.37
  280.3 1.3 copy.38
  281.6 59.5 %all-gather.11.cloned.1.call-done = bf16[2048,1024]{0,1:T(8,128)(2,1)} async-done(((bf16[256,1024]{0,1:T(8,128)(2,1)}), bf16[2048,1024]{0,1:T(8,128)(2,1)}) %all-gather.11.cloned.1.call-update) | async-done | bytes 4194320 | tf_op jit(solution)/shard_map/all_gather | solution.py:156
  341.1 6.4 %copy.39 = bf16[1,2048,1024]{2,1,0:T(8,128)(2,1)} copy(bf16[1,2048,1024]{1,2,0:T(8,128)(2,1)} %bitcast.102) | data formatting | bytes 8388608
  (2 shorter events, 0.0 us)
Async XLA Ops:
  7.2 4.3 %copy-start = (bf16[1,1024,1024]{2,1,0:T(8,128)(2,1)S(1)}, bf16[1,1024,1024]{2,1,0:T(8,128)(2,1)}, u32[]{:S(2)}) copy-start(bf16[1,1024,1024]{2,1,0:T(8,128)(2,1)} %param.11) | copy-start | bytes 6291460
  7.2 27.7 %all-gather.5.cloned.1.call-start = ((), (), s32[]{:S(2)}) async-start(), calls=%async_computation.3 | async-start | bytes 2621440 | tf_op jit(solution)/shard_map/all_gather | solution.py:129
  7.9 5.5 %copy-start.3 = (s32[1,1024]{1,0:T(1,128)S(1)}, s32[1,1024]{1,0:T(1,128)}, u32[]{:S(2)}) copy-start(s32[1,1024]{1,0:T(1,128)} %param.12) | copy-start | bytes 12292
  34.9 19.1 %copy-start.1 = (bf16[128,8,8,128]{3,2,1,0:T(8,128)(2,1)S(1)}, bf16[128,8,8,128]{3,2,1,0:T(8,128)(2,1)}, u32[]{:S(2)}) copy-start(bf16[128,8,8,128]{3,2,1,0:T(8,128)(2,1)} %copy.44) | copy-start | bytes 6291460
  114.8 9.4 %all-to-all-start = ((bf16[4,256,128]{1,2,0:T(8,128)(2,1)}), bf16[4,256,128]{1,2,0:T(8,128)(2,1)S(1)}, u32[]{:S(2)}, u32[]{:S(2)}) async-start(bf16[4,256,128]{1,2,0:T(8,128)(2,1)} %copy.32), calls=%async_computation | async-start | bytes 524288 | tf_op jit(solution)/shard_map/all_to_all | solution.py:106
  118.3 36.0 %all-gather.7.cloned.1.call-start = ((), (), s32[]{:S(2)}) async-start(), calls=%async_computation.4 | async-start | bytes 1310720 | tf_op jit(solution)/shard_map/all_gather | solution.py:111
  125.1 39.6 %all-gather.9.cloned.1.call-start = ((), (), s32[]{:S(2)}) async-start(), calls=%async_computation.5 | async-start | bytes 1310720 | tf_op jit(solution)/shard_map/all_gather | solution.py:100
  147.7 116.4 %reduce-scatter.2.cloned.1.call-start = ((), (), s32[]{:S(2)}) async-start(), calls=%async_computation.6 | async-start | bytes 4718592 | tf_op jit(solution)/shard_map/reduce_scatter | solution.py:150
  175.3 1.2 copy-start.2
  175.3 165.8 %all-gather.11.cloned.1.call-start = ((), (), s32[]{:S(2)}) async-start(), calls=%async_computation.7 | async-start | bytes 4718592 | tf_op jit(solution)/shard_map/all_gather | solution.py:156
Sparse Core Ops, SparseCore 0:
  9.5 25.2 all-gather.4
  125.2 16.8 all-gather.6
  147.8 16.8 all-gather.8
  175.4 88.6 reduce-scatter.1
  266.8 74.2 all-gather.10
where the time goes:
time: 355 us; the launch traced here: 354 us
  waiting for transfers between devices  183 us (52%)
  matrix products  83.6 us (24%)
  other arithmetic  31.9 us (9%)
  local copies, waits for them, and re-layouts  29 us (8%)
  between operations  13.9 us (4%)
  blocking collectives  9.07 us (3%)
  starting transfers between devices  3.79 us (1%)
    reduce_scatter x1, waiting for transfers between devices, body(): lax.psum_scatter(island_terms.astype(jnp.bfloat16), 'island', scatter_dim...  85.8 us
    all_gather x1, waiting for transfers between devices, body(): lax.all_gather(new_outer.astype(jnp.bfloat16), 'island', axis=0, tiled=True)  59.5 us
    convert_element_type x1, other arithmetic, score_part(): dscores = (attn_probs * (dprobs - row_dot)).astype(jnp.bfloat16)  27.9 us
    unnamed x17, local copies, waits for them, and re-layouts  27.8 us
    dot_general x1, matrix products, score_part(): jnp.einsum('qhd,kd->hqk', grad_rows, value_cols, preferred_element_type=j...  21.3 us
    all_gather x1, waiting for transfers between devices, body(): gathered = lax.all_gather(keys_values, 'mp', axis=1, tiled=True)[0]  20.8 us
    sub x1, matrix products, attention_probs(): shifted = scores - jnp.max(scores, axis=-1, keepdims=True)  19.1 us
    dot_general x1, matrix products, value_part(): jnp.einsum('hqk,qhd->kd', probs_low, grad_rows, preferred_element_type=jn...  13.3 us
  transfers between devices with their start and end apart: 6, of which 5 were waited for; matrix products, arithmetic and copies ran while one was open for 12% of the time, Pallas kernels for 0%

commit v1 on v0

--- a/solution.py
+++ b/solution.py
@@ -153,7 +153,14 @@
     outer_grad = -(reduced / island_count)
     new_momentum = MOMENTUM * momentum[0] + outer_grad
     new_outer = outer_weights[0] - OUTER_LR * (outer_grad + MOMENTUM * new_momentum)
-    next_weights = lax.all_gather(new_outer.astype(jnp.bfloat16), "island", axis=0, tiled=True)
+    value = new_outer.astype(jnp.bfloat16)
+    ways, here, hop = (lax.axis_size("island"), lax.axis_index("island"), value.shape[0])
+    dims = [n * ways if d == 0 else n for d, n in enumerate(value.shape)]
+    full = lax.dynamic_update_slice_in_dim(jnp.zeros(dims, value.dtype), value, here * hop, axis=0)
+    for far in range(1, ways):
+        value = lax.ppermute(value, "island", [(d, (d + 1) % ways) for d in range(ways)])
+        full = lax.dynamic_update_slice_in_dim(full, value, (here - far) % ways * hop, axis=0)
+    next_weights = full
     query_out = query_grads.reshape(tok_count, local_heads * head_dim)
     return (query_out[None], new_outer[None], new_momentum[None], next_weights[None])
 

time: 355 us -> 381 us (1.073)
  waiting for transfers between devices: 183 us -> 197 us
  local copies, waits for them, and re-layouts: 29 us -> 39.1 us
    ppermute x0 -> x7, waiting for transfers between devices: none -> 74 us  [body(): lax.ppermute(value, 'island', [(d, (d + 1) % ways) for d in range(ways)])]
    all_gather x1 -> x0, waiting for transfers between devices: 59.5 us -> none  [body(): lax.all_gather(new_outer.astype(jnp.bfloat16), 'island', axis=0, tiled=True)]
    broadcast_in_dim x0 -> x9, local copies, waits for them, and re-layouts: none -> 7.31 us  [body(): next_weights[None]]
    dynamic_update_slice x0 -> x8, local copies, waits for them, and re-layouts: none -> 6.66 us  [the longest x7 5.84 us: body(): lax.dynamic_update_slice_in_dim(full, value, (here - far) % ways * hop, a...]
    unnamed x17 -> x34, local copies, waits for them, and re-layouts: 27.8 us -> 23.8 us
  transfers between devices with their start and end apart: 6 -> 12, of which waited for: 5 -> 10; matrix products, arithmetic and copies ran while one was open for 12% -> 15% of each run, Pallas kernels for 0% -> 0%
where the time goes in v1:
time: 381 us; the launch traced here: 380 us
  waiting for transfers between devices  197 us (52%)
  matrix products  83.6 us (22%)
  local copies, waits for them, and re-layouts  39.1 us (10%)
  other arithmetic  31.8 us (8%)
  between operations  14.1 us (4%)
  blocking collectives  9.06 us (2%)
  starting transfers between devices  5.29 us (1%)
    reduce_scatter x1, waiting for transfers between devices, body(): lax.psum_scatter(island_terms.astype(jnp.bfloat16), 'island', scatter_dim...  85.8 us
    ppermute x7, waiting for transfers between devices, body(): lax.ppermute(value, 'island', [(d, (d + 1) % ways) for d in range(ways)])  74 us
    convert_element_type x1, other arithmetic, score_part(): dscores = (attn_probs * (dprobs - row_dot)).astype(jnp.bfloat16)  27.9 us
    unnamed x34, local copies, waits for them, and re-layouts  23.8 us
    dot_general x1, matrix products, score_part(): jnp.einsum('qhd,kd->hqk', grad_rows, value_cols, preferred_element_type=j...  21.3 us
    all_gather x1, waiting for transfers between devices, body(): gathered = lax.all_gather(keys_values, 'mp', axis=1, tiled=True)[0]  20.8 us
    sub x1, matrix products, attention_probs(): shifted = scores - jnp.max(scores, axis=-1, keepdims=True)  19.1 us
    dot_general x1, matrix products, value_part(): jnp.einsum('hqk,qhd->kd', probs_low, grad_rows, preferred_element_type=jn...  13.3 us
  transfers between devices with their start and end apart: 12, of which 10 were waited for; matrix products, arithmetic and copies ran while one was open for 15% of the time, Pallas kernels for 0%

profile of v1, /device:TPU:0, one launch (start us, length us, event | category | flops | bytes accessed | tf_op | source)
XLA Modules:
  0.0 380.1 jit_solution(6668506397362982070)
XLA Ops:
  7.2 0.0 all-gather.4.cloned.1.call-start
  7.2 0.7 all-gather.4.cloned.1.call-update
  7.9 3.5 copy.57
  11.5 1.9 copy.58
  13.4 0.6 fusion.12
  14.1 20.8 %all-gather.4.cloned.1.call-done = bf16[1,1024,1024]{2,1,0:T(8,128)(2,1)} async-done(((bf16[1,256,1024]{2,1,0:T(8,128)(2,1)}), bf16[1,1024,1024]{2,1,0:T(8,128)(2,1)}) %all-gather.4.cloned.1.call-update) | async-done | bytes 2097168 | tf_op jit(solution)/shard_map/all_gather | solution.py:129
  34.9 19.1 %fusion.73 = (f32[8,1024]{1,0:T(8,128)S(1)}, f32[8,1024,1024]{1,2,0:T(8,128)}) fusion(pred[1024,1024]{0,1:T(8,128)(4,1)S(1)} %fusion.12, bf16[1024,8,128]{2,1,0:T(8,128)(2,1)} %bitcast.114, bf16[1,1024,1024]{2,1,0:T(8,128)(2,1)} %all-gather.4.cloned.1.call-done, s32[]{:T(128)S(6)} %select_n.74), kind=kOutput, calls=%fused_computation.75 | convolution fusion | flops 2181039104 | bytes 36995076 | tf_op jit(solution)/shard_map/sub | solution.py:50
  53.9 21.3 %fusion.1 = (f32[8,1024]{1,0:T(8,128)S(1)}, f32[1024,1024,8]{1,0,2:T(8,128)}) fusion(f32[8,1024,1024]{1,2,0:T(8,128)} %get-tuple-element.20, f32[8,1024]{1,0:T(8,128)S(1)} %get-tuple-element.19, bf16[1024,8,128]{2,1,0:T(8,128)(2,1)S(1)} %bitcast.112, bf16[1,1024,1024]{2,1,0:T(8,128)(2,1)} %all-gather.4.cloned.1.call-done, s32[]{:T(128)S(6)} %select_n.76), kind=kOutput, calls=%fused_computation.3 | convolution fusion | flops 2172641280 | bytes 69533696 | tf_op jit(solution)/shard_map/qhd,kd->hqk/dot_general | solution.py:61
  75.2 27.9 %fusion.3 = bf16[8,1024,1024]{1,2,0:T(8,128)(2,1)} fusion(f32[1024,1024,8]{1,0,2:T(8,128)} %get-tuple-element.22, f32[8,1024]{1,0:T(8,128)S(1)} %get-tuple-element.21, f32[8,1024,1024]{1,2,0:T(8,128)} %get-tuple-element.20, f32[8,1024]{1,0:T(8,128)S(1)} %get-tuple-element.19), kind=kLoop, calls=%fused_computation.5 | loop fusion | flops 33554432 | bytes 83951616 | tf_op jit(solution)/shard_map/convert_element_type | solution.py:63
  103.1 10.8 %fusion.41 = bf16[1024,128]{1,0:T(8,128)(2,1)S(1)} fusion(bf16[8,1024,1024]{1,2,0:T(8,128)(2,1)} %fusion.3, bf16[1024,8,128]{2,1,0:T(8,128)(2,1)} %bitcast.115), kind=kOutput, calls=%fused_computation.36 | convolution fusion | flops 2147745792 | bytes 19136512 | tf_op jit(solution)/shard_map/hqk,qhd->kd/dot_general | solution.py:69
  114.0 0.9 copy.39
  114.8 3.4 all-to-all-start
  118.3 0.2 all-gather.6.cloned.1.call-start
  118.5 0.1 iota_multiply_fusion
  118.6 0.2 dynamic-slice_cosine_fusion
  118.8 5.4 %all-to-all-done = bf16[4,256,128]{1,2,0:T(8,128)(2,1)S(1)} async-done(((bf16[4,256,128]{1,2,0:T(8,128)(2,1)}), bf16[4,256,128]{1,2,0:T(8,128)(2,1)S(1)}, u32[]{:S(2)}, u32[]{:S(2)}) %all-to-all-start) | async-done | bytes 262176 | tf_op jit(solution)/shard_map/all_to_all | solution.py:106
  124.3 0.1 add_convert_fusion
  124.3 0.7 pad_maximum_fusion
  125.1 0.0 all-gather.8.cloned.1.call-start
  125.1 13.3 %fusion.44 = bf16[1024,128]{1,0:T(8,128)(2,1)S(1)} fusion(bf16[1024,8,128]{2,1,0:T(8,128)(2,1)S(1)} %bitcast.113, f32[8,1024,1024]{1,2,0:T(8,128)} %get-tuple-element.20, f32[8,1024]{1,0:T(8,128)S(1)} %get-tuple-element.19), kind=kOutput, calls=%fused_computation.37 | convolution fusion | flops 2164391936 | bytes 35946496 | tf_op jit(solution)/shard_map/hqk,qhd->kd/dot_general | solution.py:57
  138.5 0.1 copy.41
  138.6 9.1 %all_to_all.18 = bf16[4,256,128]{1,2,0:T(8,128)(2,1)} all-to-all(bf16[4,256,128]{1,2,0:T(8,128)(2,1)S(1)} %copy.41), channel_id=1, replica_groups=mesh['island'=8,'mp'=4] {'mp'}, dimensions={0} | all-to-all | bytes 524288 | tf_op jit(solution)/shard_map/all_to_all | solution.py:96
  147.7 0.0 all-gather.8.cloned.1.call-update
  147.7 0.0 reduce-scatter.2.cloned.1.call-start
  147.8 6.4 %copy.37 = bf16[1,2048,1024]{1,2,0:T(8,128)(2,1)} copy(bf16[1,2048,1024]{2,1,0:T(8,128)(2,1)} %param.13) | data formatting | bytes 8388608 | tf_op args[5]
  154.2 10.5 %all-gather.8.cloned.1.call-done = bf16[1024,512]{0,1:T(8,128)(2,1)} async-done(((bf16[256,512]{0,1:T(8,128)(2,1)}), bf16[1024,512]{0,1:T(8,128)(2,1)}) %all-gather.8.cloned.1.call-update) | async-done | bytes 1048592 | tf_op jit(solution)/shard_map/all_gather | solution.py:100
  164.7 10.6 %fusion.10 = bf16[2048,1024]{0,1:T(8,128)(2,1)} fusion(bf16[1,2048,1024]{1,2,0:T(8,128)(2,1)} %copy.37, bf16[1,1024,2048]{2,1,0:T(8,128)(2,1)} %param.8, bf16[1024,512]{0,1:T(8,128)(2,1)} %all-gather.8.cloned.1.call-done, bf16[1024,512]{0,1:T(8,128)(2,1)} %all-gather.6.cloned.1.call-done), kind=kOutput, calls=%fused_computation.16 | convolution fusion | flops 4307550208 | bytes 14680064 | tf_op jit(solution)/shard_map/dot_general | solution.py:86
  175.3 1.2 copy-done.3
  176.5 0.3 copy.36
  176.8 1.6 copy.42
  178.4 85.8 %reduce-scatter.2.cloned.1.call-done = bf16[256,1024]{0,1:T(8,128)(2,1)} async-done(((bf16[2048,1024]{0,1:T(8,128)(2,1)}), bf16[256,1024]{0,1:T(8,128)(2,1)}) %reduce-scatter.2.cloned.1.call-update) | async-done | bytes 524304 | tf_op jit(solution)/shard_map/reduce_scatter | solution.py:150
  264.2 2.3 fusion.71
  266.5 0.8 copy-done
  267.3 1.5 collective-permute-start
  268.7 14.5 %collective-permute-done = bf16[256,1024]{0,1:T(8,128)(2,1)S(1)} collective-permute-done((bf16[256,1024]{0,1:T(8,128)(2,1)S(1)}, bf16[256,1024]{0,1:T(8,128)(2,1)S(1)}, u32[]{:S(2)}, u32[]{:S(2)}) %collective-permute-start) | collective-permute-done | bytes 524320 | tf_op jit(solution)/shard_map/ppermute | solution.py:161
  283.2 0.8 copy-done.8
  284.0 14.3 %collective-permute-done.1 = bf16[256,1024]{0,1:T(8,128)(2,1)S(1)} collective-permute-done((bf16[256,1024]{0,1:T(8,128)(2,1)S(1)}, bf16[256,1024]{0,1:T(8,128)(2,1)S(1)}, u32[]{:S(2)}, u32[]{:S(2)}) %collective-permute-start.1) | collective-permute-done | bytes 524320 | tf_op jit(solution)/shard_map/ppermute | solution.py:161
  298.4 14.3 %collective-permute-done.2 = bf16[256,1024]{0,1:T(8,128)(2,1)S(1)} collective-permute-done((bf16[256,1024]{0,1:T(8,128)(2,1)S(1)}, bf16[256,1024]{0,1:T(8,128)(2,1)S(1)}, u32[]{:S(2)}, u32[]{:S(2)}) %collective-permute-start.2) | collective-permute-done | bytes 524320 | tf_op jit(solution)/shard_map/ppermute | solution.py:161
  312.6 0.8 copy-done.4
  313.4 13.4 %collective-permute-done.3 = bf16[256,1024]{0,1:T(8,128)(2,1)S(1)} collective-permute-done((bf16[256,1024]{0,1:T(8,128)(2,1)S(1)}, bf16[256,1024]{0,1:T(8,128)(2,1)S(1)}, u32[]{:S(2)}, u32[]{:S(2)}) %collective-permute-start.3) | collective-permute-done | bytes 524320 | tf_op jit(solution)/shard_map/ppermute | solution.py:161
  327.0 12.5 %collective-permute-done.4 = bf16[256,1024]{0,1:T(8,128)(2,1)} collective-permute-done((bf16[256,1024]{0,1:T(8,128)(2,1)S(1)}, bf16[256,1024]{0,1:T(8,128)(2,1)}, u32[]{:S(2)}, u32[]{:S(2)}) %collective-permute-start.4) | collective-permute-done | bytes 524320 | tf_op jit(solution)/shard_map/ppermute | solution.py:161
  339.5 8.5 %multiply_convert_fusion = bf16[128,8,1024]{2,0,1:T(8,128)(2,1)S(1)} fusion(bf16[8,1024,1024]{1,2,0:T(8,128)(2,1)} %fusion.3, bf16[1,1024,1024]{2,1,0:T(8,128)(2,1)} %all-gather.4.cloned.1.call-done, s32[]{:T(128)S(6)} %select_n.74), kind=kOutput, calls=%fused_computation.18 | convolution fusion | flops 2149580800 | bytes 19136516 | tf_op jit(solution)/shard_map/hqk,kd->qhd/dot_general | solution.py:65
  348.0 2.6 copy.51
  350.6 1.2 copy.43
  351.9 2.5 copy.52
  354.4 1.3 copy.53
  355.7 2.5 broadcast_in_dim.52
  358.2 0.8 constant_dynamic-update-slice_fusion.6
  359.1 0.2 copy.44
  359.3 0.8 constant_dynamic-update-slice_fusion.5
  360.1 0.2 copy.45
  360.3 0.1 collective-permute-start.6
  360.4 0.8 constant_dynamic-update-slice_fusion.4
  361.2 0.2 copy.46
  361.5 0.8 constant_dynamic-update-slice_fusion.3
  362.3 0.2 copy.47
  362.5 0.8 constant_dynamic-update-slice_fusion.2
  363.3 1.2 copy.48
  364.6 0.8 constant_dynamic-update-slice_fusion.1
  365.4 1.2 copy.49
  366.7 0.8 constant_dynamic-update-slice_fusion
  367.5 5.0 %collective-permute-done.6 = bf16[256,1024]{0,1:T(8,128)(2,1)S(1)} collective-permute-done((bf16[256,1024]{0,1:T(8,128)(2,1)}, bf16[256,1024]{0,1:T(8,128)(2,1)S(1)}, u32[]{:S(2)}, u32[]{:S(2)}) %collective-permute-start.6) | collective-permute-done | bytes 524320 | tf_op jit(solution)/shard_map/ppermute | solution.py:161
  372.5 0.2 copy.50
  372.7 0.8 constant_dynamic-update-slice_fusion.7
  (33 shorter events, 0.1 us)
Async XLA Ops:
  7.2 4.3 %copy-start.1 = (bf16[1,1024,1024]{2,1,0:T(8,128)(2,1)S(1)}, bf16[1,1024,1024]{2,1,0:T(8,128)(2,1)}, u32[]{:S(2)}) copy-start(bf16[1,1024,1024]{2,1,0:T(8,128)(2,1)} %param.11) | copy-start | bytes 6291460
  7.2 27.7 %all-gather.4.cloned.1.call-start = ((), (), s32[]{:S(2)}) async-start(), calls=%async_computation.3 | async-start | bytes 2621440 | tf_op jit(solution)/shard_map/all_gather | solution.py:129
  7.9 5.5 %copy-start.12 = (s32[1,1024]{1,0:T(1,128)S(1)}, s32[1,1024]{1,0:T(1,128)}, u32[]{:S(2)}) copy-start(s32[1,1024]{1,0:T(1,128)} %param.12) | copy-start | bytes 12292
  34.9 19.1 %copy-start.2 = (bf16[128,8,8,128]{3,2,1,0:T(8,128)(2,1)S(1)}, bf16[128,8,8,128]{3,2,1,0:T(8,128)(2,1)}, u32[]{:S(2)}) copy-start(bf16[128,8,8,128]{3,2,1,0:T(8,128)(2,1)} %copy.58) | copy-start | bytes 6291460
  114.8 9.4 %all-to-all-start = ((bf16[4,256,128]{1,2,0:T(8,128)(2,1)}), bf16[4,256,128]{1,2,0:T(8,128)(2,1)S(1)}, u32[]{:S(2)}, u32[]{:S(2)}) async-start(bf16[4,256,128]{1,2,0:T(8,128)(2,1)} %copy.39), calls=%async_computation | async-start | bytes 524288 | tf_op jit(solution)/shard_map/all_to_all | solution.py:106
  118.3 36.0 %all-gather.6.cloned.1.call-start = ((), (), s32[]{:S(2)}) async-start(), calls=%async_computation.4 | async-start | bytes 1310720 | tf_op jit(solution)/shard_map/all_gather | solution.py:111
  125.1 39.6 %all-gather.8.cloned.1.call-start = ((), (), s32[]{:S(2)}) async-start(), calls=%async_computation.5 | async-start | bytes 1310720 | tf_op jit(solution)/shard_map/all_gather | solution.py:100
  147.7 116.4 %reduce-scatter.2.cloned.1.call-start = ((), (), s32[]{:S(2)}) async-start(), calls=%async_computation.6 | async-start | bytes 4718592 | tf_op jit(solution)/shard_map/reduce_scatter | solution.py:150
  175.3 1.2 copy-start.3
  266.5 0.8 copy-start
  267.3 16.0 %collective-permute-start = (bf16[256,1024]{0,1:T(8,128)(2,1)S(1)}, bf16[256,1024]{0,1:T(8,128)(2,1)S(1)}, u32[]{:S(2)}, u32[]{:S(2)}) collective-permute-start(bf16[256,1024]{0,1:T(8,128)(2,1)S(1)} %get-tuple-element.12), channel_id=1, source_target_pairs={{0,4},{4,8},{8,12},{12,16},{16,20},{20,24},{24,28},{28,0},{1,5},{5... | collective-permute-start | bytes 1572872 | tf_op jit(solution)/shard_map/ppermute | solution.py:161
  283.2 0.8 copy-start.8
  283.2 15.1 %collective-permute-start.1 = (bf16[256,1024]{0,1:T(8,128)(2,1)S(1)}, bf16[256,1024]{0,1:T(8,128)(2,1)S(1)}, u32[]{:S(2)}, u32[]{:S(2)}) collective-permute-start(bf16[256,1024]{0,1:T(8,128)(2,1)S(1)} %collective-permute-done), channel_id=1, source_target_pairs={{0,4},{4,8},{8,12},{12,16},{16,20},{20,24},{24,28},{28,0},{1,5},{5... | collective-permute-start | bytes 1572872 | tf_op jit(solution)/shard_map/ppermute | solution.py:161
  298.4 28.5 %copy-start.10 = (bf16[256,1024]{0,1:T(8,128)(2,1)}, bf16[256,1024]{0,1:T(8,128)(2,1)S(1)}, u32[]{:S(2)}) copy-start(bf16[256,1024]{0,1:T(8,128)(2,1)S(1)} %collective-permute-done.1) | copy-start | bytes 1572868
  298.4 14.3 %collective-permute-start.2 = (bf16[256,1024]{0,1:T(8,128)(2,1)S(1)}, bf16[256,1024]{0,1:T(8,128)(2,1)S(1)}, u32[]{:S(2)}, u32[]{:S(2)}) collective-permute-start(bf16[256,1024]{0,1:T(8,128)(2,1)S(1)} %collective-permute-done.1), channel_id=1, source_target_pairs={{0,4},{4,8},{8,12},{12,16},{16,20},{20,24},{24,28},{28,0},{1,5},{5... | collective-permute-start | bytes 1572872 | tf_op jit(solution)/shard_map/ppermute | solution.py:161
  312.6 0.8 copy-start.4
  313.4 13.4 %collective-permute-start.3 = (bf16[256,1024]{0,1:T(8,128)(2,1)S(1)}, bf16[256,1024]{0,1:T(8,128)(2,1)S(1)}, u32[]{:S(2)}, u32[]{:S(2)}) collective-permute-start(bf16[256,1024]{0,1:T(8,128)(2,1)S(1)} %collective-permute-done.2), channel_id=1, source_target_pairs={{0,4},{4,8},{8,12},{12,16},{16,20},{20,24},{24,28},{28,0},{1,5},{5... | collective-permute-start | bytes 1572872 | tf_op jit(solution)/shard_map/ppermute | solution.py:161
  326.8 12.7 %copy-start.6 = (bf16[256,1024]{0,1:T(8,128)(2,1)}, bf16[256,1024]{0,1:T(8,128)(2,1)S(1)}, u32[]{:S(2)}) copy-start(bf16[256,1024]{0,1:T(8,128)(2,1)S(1)} %collective-permute-done.3) | copy-start | bytes 1572868
  326.8 12.7 %collective-permute-start.4 = (bf16[256,1024]{0,1:T(8,128)(2,1)S(1)}, bf16[256,1024]{0,1:T(8,128)(2,1)}, u32[]{:S(2)}, u32[]{:S(2)}) collective-permute-start(bf16[256,1024]{0,1:T(8,128)(2,1)S(1)} %collective-permute-done.3), channel_id=1, source_target_pairs={{0,4},{4,8},{8,12},{12,16},{16,20},{20,24},{24,28},{28,0},{1,5},{5... | collective-permute-start | bytes 1572872 | tf_op jit(solution)/shard_map/ppermute | solution.py:161
  339.5 20.8 %collective-permute-start.5 = (bf16[256,1024]{0,1:T(8,128)(2,1)}, bf16[256,1024]{0,1:T(8,128)(2,1)}, u32[]{:S(2)}, u32[]{:S(2)}) collective-permute-start(bf16[256,1024]{0,1:T(8,128)(2,1)} %collective-permute-done.4), channel_id=1, source_target_pairs={{0,4},{4,8},{8,12},{12,16},{16,20},{20,24},{24,28},{28,0},{1,5},{5... | collective-permute-start | bytes 1572872 | tf_op jit(solution)/shard_map/ppermute | solution.py:161
  354.4 4.7 %copy-start.9 = (bf16[256,1024]{0,1:T(8,128)(2,1)S(1)}, bf16[256,1024]{0,1:T(8,128)(2,1)}, u32[]{:S(2)}) copy-start(bf16[256,1024]{0,1:T(8,128)(2,1)} %copy-done.8) | copy-start | bytes 1572868
  355.7 4.4 %copy-start.11 = (bf16[256,1024]{0,1:T(8,128)(2,1)S(1)}, bf16[256,1024]{0,1:T(8,128)(2,1)}, u32[]{:S(2)}) copy-start(bf16[256,1024]{0,1:T(8,128)(2,1)} %copy-done.10) | copy-start | bytes 1572868
  355.7 5.6 %copy-start.5 = (bf16[256,1024]{0,1:T(8,128)(2,1)S(1)}, bf16[256,1024]{0,1:T(8,128)(2,1)}, u32[]{:S(2)}) copy-start(bf16[256,1024]{0,1:T(8,128)(2,1)} %copy-done.4) | copy-start | bytes 1572868
  358.2 4.0 %copy-start.7 = (bf16[256,1024]{0,1:T(8,128)(2,1)S(1)}, bf16[256,1024]{0,1:T(8,128)(2,1)}, u32[]{:S(2)}) copy-start(bf16[256,1024]{0,1:T(8,128)(2,1)} %copy-done.6) | copy-start | bytes 1572868
  360.3 12.1 %collective-permute-start.6 = (bf16[256,1024]{0,1:T(8,128)(2,1)}, bf16[256,1024]{0,1:T(8,128)(2,1)S(1)}, u32[]{:S(2)}, u32[]{:S(2)}) collective-permute-start(bf16[256,1024]{0,1:T(8,128)(2,1)} %collective-permute-done.5), channel_id=1, source_target_pairs={{0,4},{4,8},{8,12},{12,16},{16,20},{20,24},{24,28},{28,0},{1,5},{5... | collective-permute-start | bytes 1572872 | tf_op jit(solution)/shard_map/ppermute | solution.py:161
Sparse Core Ops, SparseCore 0:
  9.5 25.2 all-gather.3
  125.2 16.8 all-gather.5
  147.8 16.8 all-gather.7
  175.4 88.6 reduce-scatter.1
